TPU v7x, 32 devices: a whole 2x2x4 slice. The times are simulated.
32 devices in a mesh: fsdp: 8 (over z, y), seq: 4 (over x, core).
Axes of the slice: x: 2, y: 2, z: 4, core: 2. Of those that a mesh axis runs over, the one named last changes fastest.
Arguments:
- tokens: bfloat16 [16, 1024, 1024], P('fsdp', 'seq'), may hold values from -6 to 6
- first_gain: float32 [1024], replicated, may hold values from 0.5 to 1.5
- first_shift: float32 [1024], replicated, may hold values from -1 to 1
- attention_weight: bfloat16 [1024, 3072], P('fsdp', 'seq'), may hold values from -0.25 to 0.25
- attention_bias: float32 [3072], replicated, may hold values from -1.5 to 1.5
- output_weight: bfloat16 [1024, 1024], P('fsdp', 'seq'), may hold values from -1.5 to 1.5
- output_bias: float32 [1024], replicated, may hold values from -1 to 1
- second_gain: float32 [1024], replicated, may hold values from 0.5 to 1.5
- second_shift: float32 [1024], replicated, may hold values from -1 to 1
- expand_weight: bfloat16 [1024, 4096], P('fsdp', 'seq'), may hold values from -0.1875 to 0.1875
- expand_bias: float32 [4096], replicated, may hold values from -1 to 1
- contract_weight: bfloat16 [4096, 1024], P('fsdp', 'seq'), may hold values from -0.1875 to 0.1875
- contract_bias: float32 [1024], replicated, may hold values from -1 to 1
- cotangent: bfloat16 [16, 1024, 1024], P('fsdp', 'seq'), may hold values from -6 to 6
- threshold: float32 [1], replicated, may hold values from 3 to 6
Outputs:
- block_output: bfloat16 [16, 1024, 1024], P('fsdp', 'seq')
- input_grad: float32 [16, 1024, 1024], P('fsdp', 'seq')
- grad_first_gain: float32 [1024], replicated
- grad_first_shift: float32 [1024], replicated
- grad_attention_weight: float32 [1024, 3072], P('fsdp', 'seq')
- grad_attention_bias: float32 [3072], replicated
- grad_output_weight: float32 [1024, 1024], P('fsdp', 'seq')
- grad_output_bias: float32 [1024], replicated
- grad_second_gain: float32 [1024], replicated
- grad_second_shift: float32 [1024], replicated
- grad_expand_weight: float32 [1024, 4096], P('fsdp', 'seq')
- grad_expand_bias: float32 [4096], replicated
- grad_contract_weight: float32 [4096, 1024], P('fsdp', 'seq')
- grad_contract_bias: float32 [1024], replicated
- head_peak: float32 [16], P('seq')
- clipped_weight: float32 [1024, 3072], P('fsdp', 'seq')
- clipped_bias: float32 [3072], P('seq')
All inputs are finite; a program needn't handle non-finite values.
Results may differ from a plain program's by a relative error of at most 0.018.
Values may be sent and summed in bfloat16 or wider, within the bound.
No kernel may reach another device: no remote copies, remote signals or barrier semaphores. Data moves between devices by JAX's collectives and lax.ppermute only.
A program may use at most 320 MiB of HBM per device.

v0:
```python
import jax
import jax.numpy as jnp
from jax import lax
from jax.sharding import PartitionSpec as P

D = 1024
H = 16
HD = 64
QBLK = 512


def layer_norm(values, gain, shift):
    centered = values - jnp.mean(values, axis=-1, keepdims=True)
    variance = jnp.mean(centered * centered, axis=-1, keepdims=True)
    return centered * lax.rsqrt(variance + 1e-05) * gain + shift


def gelu_tanh(values):
    return jax.nn.gelu(values, approximate=True)


def causal_mask(row_start, row_stop):
    row_ids = row_start + jnp.arange(row_stop - row_start)[:, None]
    col_ids = jnp.arange(row_stop)[None, :]
    return col_ids <= row_ids


def block_logits(query_block, keys_part, row_start, row_stop, logit_scale):
    logits = (
        jnp.einsum("nqhd,nkhd->nhqk", query_block, keys_part, preferred_element_type=jnp.float32)
        * logit_scale
    )
    return jnp.where(causal_mask(row_start, row_stop), logits, -jnp.inf)


def split_packed(packed):
    head_size = packed.shape[-1] // 3
    return (
        packed[..., :head_size],
        packed[..., head_size : 2 * head_size],
        packed[..., 2 * head_size :],
    )


def attend_forward(packed):
    queries, keys_all, values_all = split_packed(packed)
    length = packed.shape[1]
    logit_scale = queries.shape[-1] ** (-0.5)
    outputs = []
    log_sums = []
    peak_value = None
    for block_index in range(length // QBLK):
        row_start = block_index * QBLK
        row_stop = row_start + QBLK
        logits = block_logits(
            queries[:, row_start:row_stop], keys_all[:, :row_stop], row_start, row_stop, logit_scale
        )
        row_top = jnp.max(logits, axis=-1, keepdims=True)
        shifted = jnp.exp(logits - row_top)
        row_total = jnp.sum(shifted, axis=-1, keepdims=True)
        probabilities = (shifted / row_total).astype(jnp.bfloat16)
        block_out = jnp.einsum(
            "nhqk,nkhd->nqhd",
            probabilities,
            values_all[:, :row_stop],
            preferred_element_type=jnp.float32,
        )
        outputs.append(block_out.astype(jnp.bfloat16))
        log_sums.append((row_top + jnp.log(row_total))[..., 0])
        block_peak = jnp.max(row_top[..., 0], axis=-1)
        peak_value = block_peak if peak_value is None else jnp.maximum(peak_value, block_peak)
    return (jnp.concatenate(outputs, axis=1), jnp.concatenate(log_sums, axis=-1), peak_value)


def attend_items(packed):
    attended, log_sums, peak_value = attend_forward(packed)
    returned = lax.all_to_all(attended, "seq", split_axis=1, concat_axis=2, tiled=True)
    return (returned, log_sums, peak_value, packed)


def attend_backward(packed, log_sums, heads_cot):
    queries, keys_all, values_all = split_packed(packed)
    length = packed.shape[1]
    logit_scale = queries.shape[-1] ** (-0.5)
    query_grads = []
    key_grad = jnp.zeros(keys_all.shape, jnp.float32)
    value_grad = jnp.zeros(values_all.shape, jnp.float32)
    for block_index in range(length // QBLK):
        row_start = block_index * QBLK
        row_stop = row_start + QBLK
        query_block = queries[:, row_start:row_stop]
        cot_block = heads_cot[:, row_start:row_stop]
        logits = block_logits(query_block, keys_all[:, :row_stop], row_start, row_stop, logit_scale)
        probabilities = jnp.exp(logits - log_sums[:, :, row_start:row_stop, None])
        prob_grad = jnp.einsum(
            "nqhd,nkhd->nhqk",
            cot_block,
            values_all[:, :row_stop],
            preferred_element_type=jnp.float32,
        )
        row_inner = jnp.sum(prob_grad * probabilities, axis=-1, keepdims=True)
        logit_grad = (probabilities * (prob_grad - row_inner)).astype(jnp.bfloat16)
        query_grads.append(
            jnp.einsum(
                "nhqk,nkhd->nqhd",
                logit_grad,
                keys_all[:, :row_stop],
                preferred_element_type=jnp.float32,
            )
            * logit_scale
        )
        key_grad = key_grad.at[:, :row_stop].add(
            jnp.einsum(
                "nhqk,nqhd->nkhd", logit_grad, query_block, preferred_element_type=jnp.float32
            )
            * logit_scale
        )
        value_grad = value_grad.at[:, :row_stop].add(
            jnp.einsum(
                "nhqk,nqhd->nkhd",
                probabilities.astype(jnp.bfloat16),
                cot_block,
                preferred_element_type=jnp.float32,
            )
        )
    joined = jnp.concatenate([jnp.concatenate(query_grads, axis=1), key_grad, value_grad], axis=-1)
    return joined.astype(jnp.bfloat16)


def body(
    tokens,
    first_gain,
    first_shift,
    attention_weight,
    attention_bias,
    output_weight,
    output_bias,
    second_gain,
    second_shift,
    expand_weight,
    expand_bias,
    contract_weight,
    contract_bias,
    cotangent,
    threshold,
):
    partial_full = (
        lax.all_gather(attention_weight, "seq", axis=1, tiled=True),
        lax.all_gather(output_weight, "seq", axis=1, tiled=True),
        lax.all_gather(expand_weight, "seq", axis=1, tiled=True),
        lax.all_gather(contract_weight, "seq", axis=1, tiled=True),
    )
    full_weights = (
        lax.all_gather(partial_full[0], "fsdp", axis=0, tiled=True),
        lax.all_gather(partial_full[1], "fsdp", axis=0, tiled=True),
        lax.all_gather(partial_full[2], "fsdp", axis=0, tiled=True),
        lax.all_gather(partial_full[3], "fsdp", axis=0, tiled=True),
    )
    mixing_full, output_full, expand_full, contract_full = full_weights
    seq_here = tokens.shape[0]
    tok_here = tokens.shape[1]
    tokens_float = tokens.astype(jnp.float32)
    normed_first = layer_norm(tokens_float, first_gain, first_shift).astype(jnp.bfloat16)
    mixed = (
        jnp.einsum("ntd,de->nte", normed_first, mixing_full, preferred_element_type=jnp.float32)
        + attention_bias
    )
    mixed = mixed.astype(jnp.bfloat16).reshape(seq_here, tok_here, H, 3 * HD)
    returned, log_sums, peaks, packed = attend_items(
        lax.all_to_all(mixed, "seq", split_axis=2, concat_axis=1, tiled=True)
    )
    attended = returned.reshape(seq_here, tok_here, D)
    residual = (
        tokens_float
        + jnp.einsum("nte,ed->ntd", attended, output_full, preferred_element_type=jnp.float32)
        + output_bias
    )
    normed_second = layer_norm(residual, second_gain, second_shift).astype(jnp.bfloat16)
    hidden = (
        jnp.einsum("ntd,di->nti", normed_second, expand_full, preferred_element_type=jnp.float32)
        + expand_bias
    )
    active = gelu_tanh(hidden).astype(jnp.bfloat16)
    result = (
        residual
        + jnp.einsum("nti,id->ntd", active, contract_full, preferred_element_type=jnp.float32)
        + contract_bias
    )
    block_output = result.astype(jnp.bfloat16)
    cot_float = cotangent.astype(jnp.float32)
    grad_contract = jnp.einsum("nti,ntd->id", active, cotangent, preferred_element_type=jnp.float32)
    grad_contract_bias = jnp.sum(cot_float, axis=(0, 1))
    active_cot = jnp.einsum(
        "ntd,id->nti", cotangent, contract_full, preferred_element_type=jnp.float32
    )
    _, gelu_pull = jax.vjp(gelu_tanh, hidden)
    hidden_cot = gelu_pull(active_cot)[0].astype(jnp.bfloat16)
    grad_expand = jnp.einsum(
        "ntd,nti->di", normed_second, hidden_cot, preferred_element_type=jnp.float32
    )
    grad_expand_bias = jnp.sum(hidden_cot.astype(jnp.float32), axis=(0, 1))
    second_cot = jnp.einsum(
        "nti,di->ntd", hidden_cot, expand_full, preferred_element_type=jnp.float32
    )
    _, second_pull = jax.vjp(layer_norm, residual, second_gain, second_shift)
    residual_part, grad_second_gain, grad_second_shift = second_pull(second_cot)
    residual_cot = cot_float + residual_part
    branch_cot = residual_cot.astype(jnp.bfloat16)
    grad_output = jnp.einsum(
        "nte,ntd->ed", attended, branch_cot, preferred_element_type=jnp.float32
    )
    grad_output_bias = jnp.sum(branch_cot.astype(jnp.float32), axis=(0, 1))
    attended_cot = jnp.einsum(
        "ntd,ed->nte", branch_cot, output_full, preferred_element_type=jnp.float32
    )
    attended_cot = attended_cot.astype(jnp.bfloat16).reshape(seq_here, tok_here, H, HD)
    heads_cot = lax.all_to_all(attended_cot, "seq", split_axis=2, concat_axis=1, tiled=True)
    packed_cot = attend_backward(packed, log_sums, heads_cot)
    mixed_cot = lax.all_to_all(packed_cot, "seq", split_axis=1, concat_axis=2, tiled=True).reshape(
        seq_here, tok_here, 3 * D
    )
    grad_mixing = jnp.einsum(
        "ntd,nte->de", normed_first, mixed_cot, preferred_element_type=jnp.float32
    )
    grad_mixing_bias = jnp.sum(mixed_cot.astype(jnp.float32), axis=(0, 1))
    first_cot = jnp.einsum(
        "nte,de->ntd", mixed_cot, mixing_full, preferred_element_type=jnp.float32
    )
    _, first_pull = jax.vjp(layer_norm, tokens_float, first_gain, first_shift)
    token_part, grad_first_gain, grad_first_shift = first_pull(first_cot)
    input_grad = residual_cot + token_part
    summed_first = (
        lax.psum_scatter(
            grad_mixing.astype(jnp.bfloat16), "fsdp", scatter_dimension=0, tiled=True
        ).astype(jnp.float32),
        lax.psum_scatter(
            grad_output.astype(jnp.bfloat16), "fsdp", scatter_dimension=0, tiled=True
        ).astype(jnp.float32),
        lax.psum_scatter(
            grad_expand.astype(jnp.bfloat16), "fsdp", scatter_dimension=0, tiled=True
        ).astype(jnp.float32),
        lax.psum_scatter(
            grad_contract.astype(jnp.bfloat16), "fsdp", scatter_dimension=0, tiled=True
        ).astype(jnp.float32),
    )
    weight_grads = (
        lax.psum_scatter(
            summed_first[0].astype(jnp.bfloat16), "seq", scatter_dimension=1, tiled=True
        ).astype(jnp.float32),
        lax.psum_scatter(
            summed_first[1].astype(jnp.bfloat16), "seq", scatter_dimension=1, tiled=True
        ).astype(jnp.float32),
        lax.psum_scatter(
            summed_first[2].astype(jnp.bfloat16), "seq", scatter_dimension=1, tiled=True
        ).astype(jnp.float32),
        lax.psum_scatter(
            summed_first[3].astype(jnp.bfloat16), "seq", scatter_dimension=1, tiled=True
        ).astype(jnp.float32),
    )
    vector_totals = lax.psum(
        (
            grad_first_gain,
            grad_first_shift,
            grad_mixing_bias,
            grad_output_bias,
            grad_second_gain,
            grad_second_shift,
            grad_expand_bias,
            grad_contract_bias,
        ),
        ("fsdp", "seq"),
    )
    head_peak = lax.pmax(jnp.max(peaks, axis=0), "fsdp")
    rows_here = attention_weight.shape[0]
    col_width = attention_weight.shape[1]
    heads_here = head_peak.shape[0]
    head_size = col_width // (3 * heads_here)
    factor = jnp.sqrt(threshold[0] / jnp.maximum(head_peak, threshold[0]))
    multiplier = jnp.stack([factor, factor, jnp.ones_like(factor)], axis=1)
    clipped_weight = (
        attention_weight.astype(jnp.float32).reshape(rows_here, heads_here, 3, head_size)
        * multiplier[None, :, :, None]
    ).reshape(rows_here, col_width)
    bias_piece = lax.dynamic_slice_in_dim(
        attention_bias, lax.axis_index("seq") * col_width, col_width
    )
    clipped_bias = (bias_piece.reshape(heads_here, 3, head_size) * multiplier[:, :, None]).reshape(
        col_width
    )
    return (
        block_output,
        input_grad,
        vector_totals[0],
        vector_totals[1],
        weight_grads[0],
        vector_totals[2],
        weight_grads[1],
        vector_totals[3],
        vector_totals[4],
        vector_totals[5],
        weight_grads[2],
        vector_totals[6],
        weight_grads[3],
        vector_totals[7],
        head_peak,
        clipped_weight,
        clipped_bias,
    )


def solution(mesh):
    placed = (
        P("fsdp", "seq", None),
        P(),
        P(),
        P("fsdp", "seq"),
        P(),
        P("fsdp", "seq"),
        P(),
        P(),
        P(),
        P("fsdp", "seq"),
        P(),
        P("fsdp", "seq"),
        P(),
        P("fsdp", "seq", None),
        P(),
    )
    return jax.shard_map(
        body,
        mesh=mesh,
        in_specs=placed,
        out_specs=(
            P("fsdp", "seq", None),
            P("fsdp", "seq", None),
            P(),
            P(),
            P("fsdp", "seq"),
            P(),
            P("fsdp", "seq"),
            P(),
            P(),
            P(),
            P("fsdp", "seq"),
            P(),
            P("fsdp", "seq"),
            P(),
            P("seq"),
            P("fsdp", "seq"),
            P("seq"),
        ),
        check_vma=False,
    )
```

profile of v0, /device:TPU:0, one launch (start us, length us, event | category | flops | bytes accessed | tf_op | source)
XLA Modules:
  0.0 1167.2 jit_solution(12801582693143362905)
XLA Ops:
  8.8 11.7 %all_gather.24 = bf16[128,3072]{1,0:T(8,128)(2,1)} all-gather(bf16[128,768]{1,0:T(8,128)(2,1)} %param.30), channel_id=1, replica_groups=mesh['fsdp'=8,'seq'=4] {'seq'}, dimensions={1}, use_global_device_ids=true | all-gather | bytes 983040 | tf_op jit(solution)/shard_map/all_gather | solution.py:148
  20.5 8.3 all_gather.26
  30.6 18.4 %all-gather.15.cloned.1.call-done = bf16[512,1024]{1,0:T(8,128)(2,1)} async-done(((bf16[512,256]{1,0:T(8,128)(2,1)}), bf16[512,1024]{1,0:T(8,128)(2,1)}) %all-gather.15.cloned.1.call-update) | async-done | bytes 1048592 | tf_op jit(solution)/shard_map/all_gather | solution.py:151
  49.6 100.5 %all-gather.7.cloned.1.call-done = bf16[1024,3072]{1,0:T(8,128)(2,1)} async-done(((bf16[128,3072]{1,0:T(8,128)(2,1)}), bf16[1024,3072]{1,0:T(8,128)(2,1)}) %all-gather.7.cloned.1.call-update) | async-done | bytes 6291472 | tf_op jit(solution)/shard_map/all_gather | solution.py:154
  150.2 7.8 add_convert_fusion
  158.0 4.7 copy.155
  162.8 4.0 copy.156
  166.7 5.0 all-to-all-start
  172.2 36.5 %all-to-all-done = bf16[2,256,16,192]{1,3,0,2:T(8,128)(2,1)} async-done(((bf16[2,256,16,192]{1,3,0,2:T(8,128)(2,1)}), bf16[2,256,16,192]{1,3,0,2:T(8,128)(2,1)}, u32[]{:S(2)}, u32[]{:S(2)}) %all-to-all-start) | async-done | bytes 3145760 | tf_op jit(solution)/shard_map/all_to_all | solution.py:170
  208.7 6.3 copy.158
  215.0 6.1 all_to_all.51
  231.1 3.7 fusion
  236.8 4.5 fusion.73
  248.0 18.9 %all_to_all.66 = bf16[4,2,65536]{2,1,0:T(2,128)(2,1)} all-to-all(bf16[4,2,65536]{2,1,0:T(2,128)(2,1)} %reshape.309), channel_id=1, replica_groups=mesh['fsdp'=8,'seq'=4] {'seq'}, dimensions={0} | all-to-all | bytes 2097152 | tf_op jit(solution)/shard_map/all_to_all | solution.py:77
  276.3 48.9 %all-gather.13.cloned.1.call-done = bf16[1024,4096]{1,0:T(8,128)(2,1)} async-done(((bf16[128,4096]{1,0:T(8,128)(2,1)}), bf16[1024,4096]{1,0:T(8,128)(2,1)}) %all-gather.13.cloned.1.call-update) | async-done | bytes 8388624 | tf_op jit(solution)/shard_map/all_gather | solution.py:156
  325.2 10.2 fusion.17
  335.4 114.9 %all-gather.17.cloned.1.call-done = bf16[4096,1024]{1,0:T(8,128)(2,1)} async-done(((bf16[512,1024]{1,0:T(8,128)(2,1)}), bf16[4096,1024]{1,0:T(8,128)(2,1)}) %all-gather.17.cloned.1.call-update) | async-done | bytes 8388624 | tf_op jit(solution)/shard_map/all_gather | solution.py:157
  450.4 14.6 %convert_reduce_fusion = (f32[4096]{0:T(1024)}, bf16[2,256,4096]{2,1,0:T(8,128)(2,1)S(1)}) fusion(f32[2,256,4096]{2,1,0:T(8,128)} %fusion.17, f32[4096]{0:T(1024)S(1)} %copy-done.41, bf16[2,256,1024]{2,1,0:T(8,128)(2,1)} %param.40, bf16[4096,1024]{1,0:T(8,128)(2,1)} %all-gather.17.cloned.1.call-done), kind=kOutput, calls=%fused_computation.29 | convolution fusion | flops 4343197696 | bytes 22052864 | tf_op jit(solution)/shard_map/ntd,id->nti/dot_general | solution.py:193
  465.0 5.5 multiply_reduce_fusion.2
  478.8 3.5 all-to-all-start.2
  483.0 3.8 bitcast_convert_fusion.3
  486.9 9.9 all-to-all-done.2
  500.5 6.3 fusion.62
  506.7 7.6 fusion.99
  514.4 4.9 multiply_convert_fusion.1
  519.3 3.5 fusion.71
  522.8 3.4 fusion.65
  526.2 10.9 fusion.98
  537.1 7.9 multiply_convert_fusion
  545.0 4.7 fusion.72
  549.7 4.0 fusion.48
  553.8 4.4 fusion.47
  560.0 7.6 copy.170
  567.6 53.8 %all_to_all.67 = bf16[2,1024,4,192]{3,2,0,1:T(4,128)(2,1)} all-to-all(bf16[2,1024,4,192]{3,2,0,1:T(4,128)(2,1)} %copy.170), channel_id=1, replica_groups=mesh['fsdp'=8,'seq'=4] {'seq'}, dimensions={1} | all-to-all | bytes 6291456 | tf_op jit(solution)/shard_map/all_to_all | solution.py:219
  621.5 7.3 copy.172
  628.7 7.7 bitcast_convert_fusion.2
  637.7 13.1 %bitcast_convert_fusion = bf16[4096,1024]{1,0:T(8,128)(2,1)} fusion(bf16[2,256,1024]{2,1,0:T(8,128)(2,1)S(1)} %copy-done.12, f32[2,256,4096]{2,1,0:T(8,128)} %fusion.17, f32[4096]{0:T(1024)S(1)} %copy-done.42), kind=kOutput, calls=%fused_computation | convolution fusion | flops 4320133120 | bytes 17842176 | tf_op jit(solution)/shard_map/nti,ntd->id/dot_general | solution.py:191
  652.4 9.5 bitcast_convert_fusion.1
  662.7 89.2 %reduce-scatter.9.cloned.1.call-done = bf16[128,3072]{1,0:T(8,128)(2,1)} async-done(((bf16[1024,3072]{1,0:T(8,128)(2,1)}), bf16[128,3072]{1,0:T(8,128)(2,1)}) %reduce-scatter.9.cloned.1.call-update) | async-done | bytes 786448 | tf_op jit(solution)/shard_map/reduce_scatter | solution.py:233
  752.7 151.0 %reduce-scatter.21.cloned.1.call-done = bf16[512,1024]{1,0:T(8,128)(2,1)} async-done(((bf16[4096,1024]{1,0:T(8,128)(2,1)}), bf16[512,1024]{1,0:T(8,128)(2,1)}) %reduce-scatter.21.cloned.1.call-update) | async-done | bytes 1048592 | tf_op jit(solution)/shard_map/reduce_scatter | solution.py:242
  903.8 12.2 %add_convert_fusion.1 = bf16[2,256,1024]{2,1,0:T(8,128)(2,1)} fusion(f32[2,256,1024]{2,1,0:T(8,128)S(1)} %copy-done.6, bf16[4096,1024]{1,0:T(8,128)(2,1)} %all-gather.17.cloned.1.call-done, f32[1024]{0:T(1024)S(1)} %copy-done.47, f32[2,256,4096]{2,1,0:T(8,128)} %fusion.17, f32[4096]{0:T(1024)S(1)} %copy-done.42), kind=kOutput, calls=%fused_computation.83 | convolution fusion | flops 4317511680 | bytes 19943424 | tf_op jit(solution)/shard_map/nti,id->ntd/dot_general | solution.py:186
  916.0 20.6 %pmax.7 = f32[4]{0:T(128)S(1)} all-reduce(f32[4]{0:T(128)S(1)} %maximum_reduce_fusion), channel_id=1, replica_groups=mesh['fsdp'=8,'seq'=4] {'fsdp'}, use_global_device_ids=true, to_apply=%region_41.42 | all-reduce | flops 4 | bytes 32 | tf_op jit(solution)/shard_map/pmax | solution.py:273
  939.2 8.0 copy.193
  950.7 105.3 %reduce-scatter.17.cloned.1.call-done = bf16[128,4096]{1,0:T(8,128)(2,1)} async-done(((bf16[1024,4096]{1,0:T(8,128)(2,1)}), bf16[128,4096]{1,0:T(8,128)(2,1)}) %reduce-scatter.17.cloned.1.call-update) | async-done | bytes 1048592 | tf_op jit(solution)/shard_map/reduce_scatter | solution.py:239
  1056.0 7.0 fusion.100
  1066.7 40.8 %all-reduce.2 = (f32[1024]{0:T(1024)}, f32[1024]{0:T(1024)}, f32[3072]{0:T(1024)}, f32[1024]{0:T(1024)}, f32[1024]{0:T(1024)}, /*index=5*/f32[1024]{0:T(1024)}, f32[4096]{0:T(1024)}, f32[1024]{0:T(1024)}) all-reduce(f32[1024]{0:T(1024)S(1)} %get-tuple-element.87, ...), channel_id=1, replica_groups=mesh['fsdp'=8,'seq'=4] {'fsdp','seq'}, use_global_device_ids=true, to_apply=%region_15.16 | all-reduce | flops 13312 | bytes 106496 | tf_op jit(solution)/shard_map/psum | solution.py:260
  1110.7 20.5 %reduce-scatter.23.cloned.1.call-done = bf16[512,256]{1,0:T(8,128)(2,1)} async-done(((bf16[512,1024]{1,0:T(8,128)(2,1)}), bf16[512,256]{1,0:T(8,128)(2,1)}) %reduce-scatter.23.cloned.1.call-update) | async-done | bytes 262160 | tf_op jit(solution)/shard_map/reduce_scatter | solution.py:256
  1133.0 25.7 %reduce-scatter.19.cloned.1.call-done = bf16[128,1024]{1,0:T(8,128)(2,1)} async-done(((bf16[128,4096]{1,0:T(8,128)(2,1)}), bf16[128,1024]{1,0:T(8,128)(2,1)}) %reduce-scatter.19.cloned.1.call-update) | async-done | bytes 262160 | tf_op jit(solution)/shard_map/reduce_scatter | solution.py:253
  (199 shorter events, 67.3 us)
Async XLA Ops:
  7.2 41.8 %copy-start.2 = (bf16[2,256,1024]{2,1,0:T(8,128)(2,1)S(1)}, bf16[2,256,1024]{2,1,0:T(8,128)(2,1)}, u32[]{:S(2)}) copy-start(bf16[2,256,1024]{2,1,0:T(8,128)(2,1)} %param.27) | copy-start | bytes 3145732
  7.2 143.0 %copy-start.28 = (f32[1024]{0:T(1024)S(1)}, f32[1024]{0:T(1024)}, u32[]{:S(2)}) copy-start(f32[1024]{0:T(1024)} %param.28) | copy-start | bytes 12292
  7.2 143.0 %copy-start.39 = (f32[3072]{0:T(1024)S(1)}, f32[3072]{0:T(1024)}, u32[]{:S(2)}) copy-start(f32[3072]{0:T(1024)} %param.31) | copy-start | bytes 36868
  7.2 143.0 %copy-start.43 = (f32[1024]{0:T(1024)S(1)}, f32[1024]{0:T(1024)}, u32[]{:S(2)}) copy-start(f32[1024]{0:T(1024)} %param.29) | copy-start | bytes 12292
  7.2 23.3 %all-gather.11.cloned.1.call-start = ((), (), s32[]{:S(2)}) async-start(), calls=%async_computation.14 | async-start | bytes 1310720 | tf_op jit(solution)/shard_map/all_gather | solution.py:150
  8.0 41.0 %all-gather.15.cloned.1.call-start = ((), (), s32[]{:S(2)}) async-start(), calls=%async_computation.16 | async-start | bytes 1310720 | tf_op jit(solution)/shard_map/all_gather | solution.py:151
  8.7 141.5 %all-gather.7.cloned.1.call-start = ((), (), s32[]{:S(2)}) async-start(), calls=%async_computation.12 | async-start | bytes 7077888 | tf_op jit(solution)/shard_map/all_gather | solution.py:154
  20.5 252.2 %all-gather.9.cloned.1.call-start = ((), (), s32[]{:S(2)}) async-start(), calls=%async_computation.13 | async-start | bytes 2359296 | tf_op jit(solution)/shard_map/all_gather | solution.py:155
  28.9 296.4 %all-gather.13.cloned.1.call-start = ((), (), s32[]{:S(2)}) async-start(), calls=%async_computation.15 | async-start | bytes 9437184 | tf_op jit(solution)/shard_map/all_gather | solution.py:156
  30.5 419.8 %all-gather.17.cloned.1.call-start = ((), (), s32[]{:S(2)}) async-start(), calls=%async_computation.17 | async-start | bytes 9437184 | tf_op jit(solution)/shard_map/all_gather | solution.py:157
  49.2 108.8 %copy-start.21 = (f32[2,256]{1,0:T(2,128)}, f32[2,256]{1,0:T(2,128)S(1)}, u32[]{:S(2)}) copy-start(f32[2,256]{1,0:T(2,128)S(1)} %broadcast_multiply_fusion.1) | copy-start | bytes 6148
  49.6 108.4 %copy-start.25 = (f32[2,256]{1,0:T(2,128)}, f32[2,256]{1,0:T(2,128)S(1)}, u32[]{:S(2)}) copy-start(f32[2,256]{1,0:T(2,128)S(1)} %fusion.44) | copy-start | bytes 6148
  49.6 108.4 %copy-start.23 = (f32[2,256]{1,0:T(2,128)}, f32[2,256]{1,0:T(2,128)S(1)}, u32[]{:S(2)}) copy-start(f32[2,256]{1,0:T(2,128)S(1)} %fusion.96) | copy-start | bytes 6148
  166.7 42.0 %all-to-all-start = ((bf16[2,256,16,192]{1,3,0,2:T(8,128)(2,1)}), bf16[2,256,16,192]{1,3,0,2:T(8,128)(2,1)}, u32[]{:S(2)}, u32[]{:S(2)}) async-start(bf16[2,256,16,192]{1,3,0,2:T(8,128)(2,1)} %copy.156), calls=%async_computation | async-start | bytes 6291456 | tf_op jit(solution)/shard_map/all_to_all | solution.py:170
  223.8 11.0 copy-start.1
  248.0 24.6 %copy-start.27 = (f32[1024]{0:T(1024)S(1)}, f32[1024]{0:T(1024)}, u32[]{:S(2)}) copy-start(f32[1024]{0:T(1024)} %param.33) | copy-start | bytes 12292
  272.6 52.6 %copy-start.37 = (f32[1024]{0:T(1024)S(1)}, f32[1024]{0:T(1024)}, u32[]{:S(2)}) copy-start(f32[1024]{0:T(1024)} %param.34) | copy-start | bytes 12292
  272.6 52.6 %copy-start.45 = (f32[1024]{0:T(1024)S(1)}, f32[1024]{0:T(1024)}, u32[]{:S(2)}) copy-start(f32[1024]{0:T(1024)} %param.35) | copy-start | bytes 12292
  275.9 194.5 %copy-start.5 = (f32[2,256,1024]{2,1,0:T(8,128)}, f32[2,256,1024]{2,1,0:T(8,128)S(1)}, u32[]{:S(2)}) copy-start(f32[2,256,1024]{2,1,0:T(8,128)S(1)} %get-tuple-element.111) | copy-start | bytes 6291460
  276.3 194.1 %copy-start.31 = (f32[2,256]{1,0:T(2,128)}, f32[2,256]{1,0:T(2,128)S(1)}, u32[]{:S(2)}) copy-start(f32[2,256]{1,0:T(2,128)S(1)} %fusion.97) | copy-start | bytes 6148
  276.3 174.0 %copy-start.41 = (f32[4096]{0:T(1024)S(1)}, f32[4096]{0:T(1024)}, u32[]{:S(2)}) copy-start(f32[4096]{0:T(1024)} %param.37) | copy-start | bytes 49156
  450.4 14.6 %copy-start.40 = (bf16[1024,4096]{1,0:T(8,128)(2,1)S(1)}, bf16[1024,4096]{1,0:T(8,128)(2,1)}, u32[]{:S(2)}) copy-start(bf16[1024,4096]{1,0:T(8,128)(2,1)} %all-gather.13.cloned.1.call-done) | copy-start | bytes 25165828
  478.8 18.0 %all-to-all-start.2 = ((bf16[2,256,16,64]{1,3,0,2:T(8,128)(2,1)}), bf16[2,256,16,64]{1,3,0,2:T(8,128)(2,1)S(1)}, u32[]{:S(2)}, u32[]{:S(2)}) async-start(bf16[2,256,16,64]{1,3,0,2:T(8,128)(2,1)} %copy.165), calls=%async_computation.2 | async-start | bytes 2097152 | tf_op jit(solution)/shard_map/all_to_all | solution.py:217
  482.3 179.7 %reduce-scatter.13.cloned.1.call-start = ((), (), s32[]{:S(2)}) async-start(), calls=%async_computation.20 | async-start | bytes 2359296 | tf_op jit(solution)/shard_map/reduce_scatter | solution.py:236
  486.8 265.1 %reduce-scatter.9.cloned.1.call-start = ((), (), s32[]{:S(2)}) async-start(), calls=%async_computation.18 | async-start | bytes 7077888 | tf_op jit(solution)/shard_map/reduce_scatter | solution.py:233
  500.5 13.9 %slice-start.4 = ((s8[8388608]{0:T(1024)(128)(4,1)}), s8[4194304]{0:T(1024)(128)(4,1)S(1)}, s32[]{:S(2)}) async-start(s8[8388608]{0:T(1024)(128)(4,1)} %bitcast.119), calls=%async_computation.30 | async-start | bytes 8388608
  506.7 7.6 slice-start.5
  514.4 11.8 %slice-start = ((s8[16777216]{0:T(1024)(128)(4,1)}), s8[4194304]{0:T(1024)(128)(4,1)S(1)}, s32[]{:S(2)}) async-start(s8[16777216]{0:T(1024)(128)(4,1)} %bitcast.117), calls=%async_computation.26 | async-start | bytes 8388608
  514.4 11.8 %slice-start.1 = ((s8[16777216]{0:T(1024)(128)(4,1)}), s8[4194304]{0:T(1024)(128)(4,1)S(1)}, s32[]{:S(2)}) async-start(s8[16777216]{0:T(1024)(128)(4,1)} %bitcast.117), calls=%async_computation.27 | async-start | bytes 8388608
  514.4 11.8 %slice-start.2 = ((s8[16777216]{0:T(1024)(128)(4,1)}), s8[4194304]{0:T(1024)(128)(4,1)S(1)}, s32[]{:S(2)}) async-start(s8[16777216]{0:T(1024)(128)(4,1)} %bitcast.117), calls=%async_computation.28 | async-start | bytes 8388608
  519.3 6.9 slice-start.3
  621.4 7.3 copy-start.22
  621.4 7.3 copy-start.24
  621.5 7.3 copy-start.29
  621.5 7.3 copy-start.44
  636.5 267.2 %reduce-scatter.21.cloned.1.call-start = ((), (), s32[]{:S(2)}) async-start(), calls=%async_computation.24 | async-start | bytes 9437184 | tf_op jit(solution)/shard_map/reduce_scatter | solution.py:242
  650.8 405.1 %reduce-scatter.17.cloned.1.call-start = ((), (), s32[]{:S(2)}) async-start(), calls=%async_computation.22 | async-start | bytes 9437184 | tf_op jit(solution)/shard_map/reduce_scatter | solution.py:239
  661.9 90.8 %copy-start.33 = (f32[2,4]{1,0:T(2,128)S(1)}, f32[2,4]{1,0:T(2,128)}, u32[]{:S(2)}) copy-start(f32[2,4]{1,0:T(2,128)} %get-tuple-element.83) | copy-start | bytes 100
  661.9 90.8 %copy-start.34 = (f32[2,4]{1,0:T(2,128)S(1)}, f32[2,4]{1,0:T(2,128)}, u32[]{:S(2)}) copy-start(f32[2,4]{1,0:T(2,128)} %get-tuple-element.81) | copy-start | bytes 100
  661.9 241.9 %copy-start.47 = (f32[1024]{0:T(1024)S(1)}, f32[1024]{0:T(1024)}, u32[]{:S(2)}) copy-start(f32[1024]{0:T(1024)} %param.39) | copy-start | bytes 12292
  661.9 445.6 %reduce-scatter.15.cloned.1.call-start = ((), (), s32[]{:S(2)}) async-start(), calls=%async_computation.21 | async-start | bytes 327680 | tf_op jit(solution)/shard_map/reduce_scatter | solution.py:250
  662.6 446.4 %reduce-scatter.11.cloned.1.call-start = ((), (), s32[]{:S(2)}) async-start(), calls=%async_computation.19 | async-start | bytes 983040 | tf_op jit(solution)/shard_map/reduce_scatter | solution.py:247
  751.9 379.3 %reduce-scatter.23.cloned.1.call-start = ((), (), s32[]{:S(2)}) async-start(), calls=%async_computation.25 | async-start | bytes 1310720 | tf_op jit(solution)/shard_map/reduce_scatter | solution.py:256
  903.7 34.6 %copy-start.19 = (bf16[128,768]{1,0:T(8,128)(2,1)S(1)}, bf16[128,768]{1,0:T(8,128)(2,1)}, u32[]{:S(2)}) copy-start(bf16[128,768]{1,0:T(8,128)(2,1)} %param.30) | copy-start | bytes 589828
  903.8 255.0 %reduce-scatter.19.cloned.1.call-start = ((), (), s32[]{:S(2)}) async-start(), calls=%async_computation.23 | async-start | bytes 1310720 | tf_op jit(solution)/shard_map/reduce_scatter | solution.py:253
  936.7 13.7 %copy-start.48 = (f32[4]{0:T(128)}, f32[4]{0:T(128)S(1)}, u32[]{:S(2)}) copy-start(f32[4]{0:T(128)S(1)} %pmax.7) | copy-start | bytes 52
  1056.0 7.0 copy-start.26
  1056.0 8.1 copy-start.13
  (24 other events, 74.5 us)
Sparse Core Ops, SparseCore 0:
  9.6 20.8 all-gather.10
  32.0 16.8 all-gather.14
  51.1 99.0 all-gather.6
  152.2 47.6 all-gather.8
  201.8 123.4 all-gather.12
  327.2 123.0 all-gather.16
  486.9 66.2 reduce-scatter.12
  636.6 115.1 reduce-scatter.8
  755.5 148.1 reduce-scatter.20
  907.6 148.2 reduce-scatter.16
  1058.4 19.0 reduce-scatter.14
  1080.1 23.4 reduce-scatter.10
  1106.1 25.0 reduce-scatter.22
  1133.8 24.9 reduce-scatter.18
where the time goes:
time: 1170 us
  waiting for transfers between devices  725 us (62%)
  blocking collectives  154 us (13%)
  matrix products  153 us (13%)
  local copies, waits for them, and re-layouts  71.4 us (6%)
  other arithmetic  39.2 us (3%)
  between operations  15.3 us (1%)
    reduce_scatter x1, waiting for transfers between devices, body(): lax.psum_scatter(grad_contract.astype(jnp.bfloat16), 'fsdp', scatter_dime...  151 us
    all_gather x1, waiting for transfers between devices, body(): lax.all_gather(partial_full[3], 'fsdp', axis=0, tiled=True)  115 us
    reduce_scatter x1, waiting for transfers between devices, body(): lax.psum_scatter(grad_expand.astype(jnp.bfloat16), 'fsdp', scatter_dimens...  105 us
    all_gather x1, waiting for transfers between devices, body(): lax.all_gather(partial_full[0], 'fsdp', axis=0, tiled=True)  101 us
    reduce_scatter x1, waiting for transfers between devices, body(): lax.psum_scatter(grad_mixing.astype(jnp.bfloat16), 'fsdp', scatter_dimens...  89.2 us
    all_to_all x1, blocking collectives, body(): lax.all_to_all(packed_cot, 'seq', split_axis=1, concat_axis=2, tiled=True)  53.8 us
    all_gather x1, waiting for transfers between devices, body(): lax.all_gather(partial_full[2], 'fsdp', axis=0, tiled=True)  48.9 us
    psum x1, blocking collectives, body(): lax.psum((grad_first_gain, grad_first_shift, grad_mixing_bias, grad_outpu...  40.8 us
  transfers between devices with their start and end apart: 16, of which 12 were waited for; matrix products, arithmetic and copies ran while one was open for 19% of the time, Pallas kernels for 0%

commit v1 on v0

--- a/solution.py
+++ b/solution.py
@@ -258,17 +258,20 @@
         ).astype(jnp.float32),
     )
     vector_totals = lax.psum(
-        (
-            grad_first_gain,
-            grad_first_shift,
-            grad_mixing_bias,
-            grad_output_bias,
-            grad_second_gain,
-            grad_second_shift,
-            grad_expand_bias,
-            grad_contract_bias,
+        lax.psum(
+            (
+                grad_first_gain,
+                grad_first_shift,
+                grad_mixing_bias,
+                grad_output_bias,
+                grad_second_gain,
+                grad_second_shift,
+                grad_expand_bias,
+                grad_contract_bias,
+            ),
+            "seq",
         ),
-        ("fsdp", "seq"),
+        "fsdp",
     )
     head_peak = lax.pmax(jnp.max(peaks, axis=0), "fsdp")
     rows_here = attention_weight.shape[0]

time: 1170 us -> 1170 us (level)
    psum x0 -> x1, blocking collectives: none -> 36.3 us  [body(): lax.psum(lax.psum((grad_first_gain, grad_first_shift, grad_mixing_bias, g...]
    psum x1, blocking collectives: 40.8 us -> 11.8 us  [body(): lax.psum((grad_first_gain, grad_first_shift, grad_mixing_bias, grad_outpu...]
where the time goes in v1:
time: 1170 us
  waiting for transfers between devices  717 us (61%)
  blocking collectives  162 us (14%)
  matrix products  153 us (13%)
  local copies, waits for them, and re-layouts  71.4 us (6%)
  other arithmetic  39.2 us (3%)
  between operations  15.3 us (1%)
    reduce_scatter x1, waiting for transfers between devices, body(): lax.psum_scatter(grad_contract.astype(jnp.bfloat16), 'fsdp', scatter_dime...  151 us
    all_gather x1, waiting for transfers between devices, body(): lax.all_gather(partial_full[3], 'fsdp', axis=0, tiled=True)  115 us
    reduce_scatter x1, waiting for transfers between devices, body(): lax.psum_scatter(grad_expand.astype(jnp.bfloat16), 'fsdp', scatter_dimens...  105 us
    all_gather x1, waiting for transfers between devices, body(): lax.all_gather(partial_full[0], 'fsdp', axis=0, tiled=True)  101 us
    reduce_scatter x1, waiting for transfers between devices, body(): lax.psum_scatter(grad_mixing.astype(jnp.bfloat16), 'fsdp', scatter_dimens...  89.1 us
    all_to_all x1, blocking collectives, body(): lax.all_to_all(packed_cot, 'seq', split_axis=1, concat_axis=2, tiled=True)  53.9 us
    all_gather x1, waiting for transfers between devices, body(): lax.all_gather(partial_full[2], 'fsdp', axis=0, tiled=True)  48.7 us
    all_to_all x1, waiting for transfers between devices, body(): lax.all_to_all(mixed, 'seq', split_axis=2, concat_axis=1, tiled=True)  36.5 us
  transfers between devices with their start and end apart: 16, of which 12 were waited for; matrix products, arithmetic and copies ran while one was open for 19% of the time, Pallas kernels for 0%

profile of v1, /device:TPU:0, one launch (start us, length us, event | category | flops | bytes accessed | tf_op | source)
XLA Modules:
  0.0 1166.8 jit_solution(2149134504588009515)
XLA Ops:
  8.8 11.7 %all_gather.24 = bf16[128,3072]{1,0:T(8,128)(2,1)} all-gather(bf16[128,768]{1,0:T(8,128)(2,1)} %param.30), channel_id=1, replica_groups=mesh['fsdp'=8,'seq'=4] {'seq'}, dimensions={1}, use_global_device_ids=true | all-gather | bytes 983040 | tf_op jit(solution)/shard_map/all_gather | solution.py:148
  20.5 8.3 all_gather.26
  30.6 18.4 %all-gather.15.cloned.1.call-done = bf16[512,1024]{1,0:T(8,128)(2,1)} async-done(((bf16[512,256]{1,0:T(8,128)(2,1)}), bf16[512,1024]{1,0:T(8,128)(2,1)}) %all-gather.15.cloned.1.call-update) | async-done | bytes 1048592 | tf_op jit(solution)/shard_map/all_gather | solution.py:151
  49.6 100.5 %all-gather.7.cloned.1.call-done = bf16[1024,3072]{1,0:T(8,128)(2,1)} async-done(((bf16[128,3072]{1,0:T(8,128)(2,1)}), bf16[1024,3072]{1,0:T(8,128)(2,1)}) %all-gather.7.cloned.1.call-update) | async-done | bytes 6291472 | tf_op jit(solution)/shard_map/all_gather | solution.py:154
  150.2 7.8 add_convert_fusion
  158.0 4.8 copy.155
  162.8 4.0 copy.156
  166.8 5.0 all-to-all-start
  172.2 36.5 %all-to-all-done = bf16[2,256,16,192]{1,3,0,2:T(8,128)(2,1)} async-done(((bf16[2,256,16,192]{1,3,0,2:T(8,128)(2,1)}), bf16[2,256,16,192]{1,3,0,2:T(8,128)(2,1)}, u32[]{:S(2)}, u32[]{:S(2)}) %all-to-all-start) | async-done | bytes 3145760 | tf_op jit(solution)/shard_map/all_to_all | solution.py:170
  208.7 6.3 copy.158
  215.1 6.1 all_to_all.51
  231.1 3.7 fusion
  236.9 4.5 fusion.73
  248.1 18.9 %all_to_all.66 = bf16[4,2,65536]{2,1,0:T(2,128)(2,1)} all-to-all(bf16[4,2,65536]{2,1,0:T(2,128)(2,1)} %reshape.309), channel_id=1, replica_groups=mesh['fsdp'=8,'seq'=4] {'seq'}, dimensions={0} | all-to-all | bytes 2097152 | tf_op jit(solution)/shard_map/all_to_all | solution.py:77
  276.4 48.7 %all-gather.13.cloned.1.call-done = bf16[1024,4096]{1,0:T(8,128)(2,1)} async-done(((bf16[128,4096]{1,0:T(8,128)(2,1)}), bf16[1024,4096]{1,0:T(8,128)(2,1)}) %all-gather.13.cloned.1.call-update) | async-done | bytes 8388624 | tf_op jit(solution)/shard_map/all_gather | solution.py:156
  325.1 10.2 fusion.17
  335.3 114.9 %all-gather.17.cloned.1.call-done = bf16[4096,1024]{1,0:T(8,128)(2,1)} async-done(((bf16[512,1024]{1,0:T(8,128)(2,1)}), bf16[4096,1024]{1,0:T(8,128)(2,1)}) %all-gather.17.cloned.1.call-update) | async-done | bytes 8388624 | tf_op jit(solution)/shard_map/all_gather | solution.py:157
  450.2 14.6 %convert_reduce_fusion = (f32[4096]{0:T(1024)}, bf16[2,256,4096]{2,1,0:T(8,128)(2,1)S(1)}) fusion(f32[2,256,4096]{2,1,0:T(8,128)} %fusion.17, f32[4096]{0:T(1024)S(1)} %copy-done.41, bf16[2,256,1024]{2,1,0:T(8,128)(2,1)} %param.40, bf16[4096,1024]{1,0:T(8,128)(2,1)} %all-gather.17.cloned.1.call-done), kind=kOutput, calls=%fused_computation.29 | convolution fusion | flops 4343197696 | bytes 22052864 | tf_op jit(solution)/shard_map/ntd,id->nti/dot_general | solution.py:193
  464.8 5.5 multiply_reduce_fusion.2
  478.7 3.5 all-to-all-start.2
  482.9 3.8 bitcast_convert_fusion.3
  486.8 9.9 all-to-all-done.2
  500.4 6.3 fusion.62
  506.7 7.6 fusion.99
  514.3 4.9 multiply_convert_fusion.1
  519.2 3.5 fusion.71
  526.1 10.9 fusion.98
  537.0 7.9 multiply_convert_fusion
  544.9 4.7 fusion.72
  549.6 4.0 fusion.48
  553.7 4.4 fusion.47
  559.9 7.6 copy.170
  567.5 53.9 %all_to_all.67 = bf16[2,1024,4,192]{3,2,0,1:T(4,128)(2,1)} all-to-all(bf16[2,1024,4,192]{3,2,0,1:T(4,128)(2,1)} %copy.170), channel_id=1, replica_groups=mesh['fsdp'=8,'seq'=4] {'seq'}, dimensions={1} | all-to-all | bytes 6291456 | tf_op jit(solution)/shard_map/all_to_all | solution.py:219
  621.4 7.3 copy.172
  628.7 7.7 bitcast_convert_fusion.2
  637.7 13.1 %bitcast_convert_fusion = bf16[4096,1024]{1,0:T(8,128)(2,1)} fusion(bf16[2,256,1024]{2,1,0:T(8,128)(2,1)S(1)} %copy-done.12, f32[2,256,4096]{2,1,0:T(8,128)} %fusion.17, f32[4096]{0:T(1024)S(1)} %copy-done.42), kind=kOutput, calls=%fused_computation | convolution fusion | flops 4320133120 | bytes 17842176 | tf_op jit(solution)/shard_map/nti,ntd->id/dot_general | solution.py:191
  652.4 9.5 bitcast_convert_fusion.1
  662.6 89.1 %reduce-scatter.9.cloned.1.call-done = bf16[128,3072]{1,0:T(8,128)(2,1)} async-done(((bf16[1024,3072]{1,0:T(8,128)(2,1)}), bf16[128,3072]{1,0:T(8,128)(2,1)}) %reduce-scatter.9.cloned.1.call-update) | async-done | bytes 786448 | tf_op jit(solution)/shard_map/reduce_scatter | solution.py:233
  752.6 151.0 %reduce-scatter.21.cloned.1.call-done = bf16[512,1024]{1,0:T(8,128)(2,1)} async-done(((bf16[4096,1024]{1,0:T(8,128)(2,1)}), bf16[512,1024]{1,0:T(8,128)(2,1)}) %reduce-scatter.21.cloned.1.call-update) | async-done | bytes 1048592 | tf_op jit(solution)/shard_map/reduce_scatter | solution.py:242
  903.7 12.2 %add_convert_fusion.1 = bf16[2,256,1024]{2,1,0:T(8,128)(2,1)} fusion(f32[2,256,1024]{2,1,0:T(8,128)S(1)} %copy-done.6, bf16[4096,1024]{1,0:T(8,128)(2,1)} %all-gather.17.cloned.1.call-done, f32[1024]{0:T(1024)S(1)} %copy-done.47, f32[2,256,4096]{2,1,0:T(8,128)} %fusion.17, f32[4096]{0:T(1024)S(1)} %copy-done.42), kind=kOutput, calls=%fused_computation.83 | convolution fusion | flops 4317511680 | bytes 19943424 | tf_op jit(solution)/shard_map/nti,id->ntd/dot_general | solution.py:186
  915.9 20.6 %pmax.7 = f32[4]{0:T(128)S(1)} all-reduce(f32[4]{0:T(128)S(1)} %maximum_reduce_fusion), channel_id=1, replica_groups=mesh['fsdp'=8,'seq'=4] {'fsdp'}, use_global_device_ids=true, to_apply=%region_49.50 | all-reduce | flops 4 | bytes 32 | tf_op jit(solution)/shard_map/pmax | solution.py:276
  939.1 7.9 copy.193
  950.5 105.3 %reduce-scatter.17.cloned.1.call-done = bf16[128,4096]{1,0:T(8,128)(2,1)} async-done(((bf16[1024,4096]{1,0:T(8,128)(2,1)}), bf16[128,4096]{1,0:T(8,128)(2,1)}) %reduce-scatter.17.cloned.1.call-update) | async-done | bytes 1048592 | tf_op jit(solution)/shard_map/reduce_scatter | solution.py:239
  1055.9 7.0 fusion.100
  1066.6 11.8 %all-reduce.3 = (f32[1024]{0:T(1024)S(1)}, f32[1024]{0:T(1024)S(1)}, f32[3072]{0:T(1024)S(1)}, f32[1024]{0:T(1024)S(1)}, f32[1024]{0:T(1024)S(1)}, /*index=5*/f3...) all-reduce(f32[1024]{0:T(1024)S(1)} %get-tuple-element.87, ...), channel_id=1, replica_groups=mesh['fsdp'=8,'seq'=4] {'seq'}, use_global_device_ids=true, to_apply=%region_15.16 | all-reduce | flops 13312 | bytes 106496 | tf_op jit(solution)/shard_map/psum | solution.py:261
  1078.4 36.3 %all-reduce.2 = (f32[1024]{0:T(1024)}, f32[1024]{0:T(1024)}, f32[3072]{0:T(1024)}, f32[1024]{0:T(1024)}, f32[1024]{0:T(1024)}, /*index=5*/f32[1024]{0:T(1024)}, f32[4096]{0:T(1024)}, f32[1024]{0:T(1024)}) all-reduce(f32[1024]{0:T(1024)S(1)} %get-tuple-element.100, ...), channel_id=1, replica_groups=mesh['fsdp'=8,'seq'=4] {'fsdp'}, use_global_device_ids=true, to_apply=%region_16.17 | all-reduce | flops 13312 | bytes 106496 | tf_op jit(solution)/shard_map/psum | solution.py:260
  1117.9 12.9 %reduce-scatter.23.cloned.1.call-done = bf16[512,256]{1,0:T(8,128)(2,1)} async-done(((bf16[512,1024]{1,0:T(8,128)(2,1)}), bf16[512,256]{1,0:T(8,128)(2,1)}) %reduce-scatter.23.cloned.1.call-update) | async-done | bytes 262160 | tf_op jit(solution)/shard_map/reduce_scatter | solution.py:256
  1132.5 25.7 %reduce-scatter.19.cloned.1.call-done = bf16[128,1024]{1,0:T(8,128)(2,1)} async-done(((bf16[128,4096]{1,0:T(8,128)(2,1)}), bf16[128,1024]{1,0:T(8,128)(2,1)}) %reduce-scatter.19.cloned.1.call-update) | async-done | bytes 262160 | tf_op jit(solution)/shard_map/reduce_scatter | solution.py:253
  (200 shorter events, 70.8 us)
Async XLA Ops:
  7.2 41.8 %copy-start.2 = (bf16[2,256,1024]{2,1,0:T(8,128)(2,1)S(1)}, bf16[2,256,1024]{2,1,0:T(8,128)(2,1)}, u32[]{:S(2)}) copy-start(bf16[2,256,1024]{2,1,0:T(8,128)(2,1)} %param.27) | copy-start | bytes 3145732
  7.2 143.0 %copy-start.28 = (f32[1024]{0:T(1024)S(1)}, f32[1024]{0:T(1024)}, u32[]{:S(2)}) copy-start(f32[1024]{0:T(1024)} %param.28) | copy-start | bytes 12292
  7.2 143.0 %copy-start.39 = (f32[3072]{0:T(1024)S(1)}, f32[3072]{0:T(1024)}, u32[]{:S(2)}) copy-start(f32[3072]{0:T(1024)} %param.31) | copy-start | bytes 36868
  7.2 143.0 %copy-start.43 = (f32[1024]{0:T(1024)S(1)}, f32[1024]{0:T(1024)}, u32[]{:S(2)}) copy-start(f32[1024]{0:T(1024)} %param.29) | copy-start | bytes 12292
  7.2 23.3 %all-gather.11.cloned.1.call-start = ((), (), s32[]{:S(2)}) async-start(), calls=%async_computation.14 | async-start | bytes 1310720 | tf_op jit(solution)/shard_map/all_gather | solution.py:150
  8.0 41.0 %all-gather.15.cloned.1.call-start = ((), (), s32[]{:S(2)}) async-start(), calls=%async_computation.16 | async-start | bytes 1310720 | tf_op jit(solution)/shard_map/all_gather | solution.py:151
  8.7 141.5 %all-gather.7.cloned.1.call-start = ((), (), s32[]{:S(2)}) async-start(), calls=%async_computation.12 | async-start | bytes 7077888 | tf_op jit(solution)/shard_map/all_gather | solution.py:154
  20.5 252.2 %all-gather.9.cloned.1.call-start = ((), (), s32[]{:S(2)}) async-start(), calls=%async_computation.13 | async-start | bytes 2359296 | tf_op jit(solution)/shard_map/all_gather | solution.py:155
  28.9 296.2 %all-gather.13.cloned.1.call-start = ((), (), s32[]{:S(2)}) async-start(), calls=%async_computation.15 | async-start | bytes 9437184 | tf_op jit(solution)/shard_map/all_gather | solution.py:156
  30.5 419.7 %all-gather.17.cloned.1.call-start = ((), (), s32[]{:S(2)}) async-start(), calls=%async_computation.17 | async-start | bytes 9437184 | tf_op jit(solution)/shard_map/all_gather | solution.py:157
  49.2 108.9 %copy-start.21 = (f32[2,256]{1,0:T(2,128)}, f32[2,256]{1,0:T(2,128)S(1)}, u32[]{:S(2)}) copy-start(f32[2,256]{1,0:T(2,128)S(1)} %broadcast_multiply_fusion.1) | copy-start | bytes 6148
  49.6 108.4 %copy-start.25 = (f32[2,256]{1,0:T(2,128)}, f32[2,256]{1,0:T(2,128)S(1)}, u32[]{:S(2)}) copy-start(f32[2,256]{1,0:T(2,128)S(1)} %fusion.44) | copy-start | bytes 6148
  49.6 108.4 %copy-start.23 = (f32[2,256]{1,0:T(2,128)}, f32[2,256]{1,0:T(2,128)S(1)}, u32[]{:S(2)}) copy-start(f32[2,256]{1,0:T(2,128)S(1)} %fusion.96) | copy-start | bytes 6148
  166.8 42.0 %all-to-all-start = ((bf16[2,256,16,192]{1,3,0,2:T(8,128)(2,1)}), bf16[2,256,16,192]{1,3,0,2:T(8,128)(2,1)}, u32[]{:S(2)}, u32[]{:S(2)}) async-start(bf16[2,256,16,192]{1,3,0,2:T(8,128)(2,1)} %copy.156), calls=%async_computation | async-start | bytes 6291456 | tf_op jit(solution)/shard_map/all_to_all | solution.py:170
  223.9 11.0 copy-start.1
  248.1 24.6 %copy-start.27 = (f32[1024]{0:T(1024)S(1)}, f32[1024]{0:T(1024)}, u32[]{:S(2)}) copy-start(f32[1024]{0:T(1024)} %param.33) | copy-start | bytes 12292
  272.7 52.4 %copy-start.37 = (f32[1024]{0:T(1024)S(1)}, f32[1024]{0:T(1024)}, u32[]{:S(2)}) copy-start(f32[1024]{0:T(1024)} %param.34) | copy-start | bytes 12292
  272.7 52.4 %copy-start.45 = (f32[1024]{0:T(1024)S(1)}, f32[1024]{0:T(1024)}, u32[]{:S(2)}) copy-start(f32[1024]{0:T(1024)} %param.35) | copy-start | bytes 12292
  276.0 194.3 %copy-start.5 = (f32[2,256,1024]{2,1,0:T(8,128)}, f32[2,256,1024]{2,1,0:T(8,128)S(1)}, u32[]{:S(2)}) copy-start(f32[2,256,1024]{2,1,0:T(8,128)S(1)} %get-tuple-element.119) | copy-start | bytes 6291460
  276.4 193.9 %copy-start.31 = (f32[2,256]{1,0:T(2,128)}, f32[2,256]{1,0:T(2,128)S(1)}, u32[]{:S(2)}) copy-start(f32[2,256]{1,0:T(2,128)S(1)} %fusion.97) | copy-start | bytes 6148
  276.4 173.8 %copy-start.41 = (f32[4096]{0:T(1024)S(1)}, f32[4096]{0:T(1024)}, u32[]{:S(2)}) copy-start(f32[4096]{0:T(1024)} %param.37) | copy-start | bytes 49156
  450.2 14.6 %copy-start.40 = (bf16[1024,4096]{1,0:T(8,128)(2,1)S(1)}, bf16[1024,4096]{1,0:T(8,128)(2,1)}, u32[]{:S(2)}) copy-start(bf16[1024,4096]{1,0:T(8,128)(2,1)} %all-gather.13.cloned.1.call-done) | copy-start | bytes 25165828
  478.7 18.0 %all-to-all-start.2 = ((bf16[2,256,16,64]{1,3,0,2:T(8,128)(2,1)}), bf16[2,256,16,64]{1,3,0,2:T(8,128)(2,1)S(1)}, u32[]{:S(2)}, u32[]{:S(2)}) async-start(bf16[2,256,16,64]{1,3,0,2:T(8,128)(2,1)} %copy.165), calls=%async_computation.2 | async-start | bytes 2097152 | tf_op jit(solution)/shard_map/all_to_all | solution.py:217
  482.2 179.7 %reduce-scatter.13.cloned.1.call-start = ((), (), s32[]{:S(2)}) async-start(), calls=%async_computation.20 | async-start | bytes 2359296 | tf_op jit(solution)/shard_map/reduce_scatter | solution.py:236
  486.7 265.1 %reduce-scatter.9.cloned.1.call-start = ((), (), s32[]{:S(2)}) async-start(), calls=%async_computation.18 | async-start | bytes 7077888 | tf_op jit(solution)/shard_map/reduce_scatter | solution.py:233
  500.4 13.9 %slice-start.4 = ((s8[8388608]{0:T(1024)(128)(4,1)}), s8[4194304]{0:T(1024)(128)(4,1)S(1)}, s32[]{:S(2)}) async-start(s8[8388608]{0:T(1024)(128)(4,1)} %bitcast.119), calls=%async_computation.30 | async-start | bytes 8388608
  506.7 7.6 slice-start.5
  514.3 11.8 %slice-start = ((s8[16777216]{0:T(1024)(128)(4,1)}), s8[4194304]{0:T(1024)(128)(4,1)S(1)}, s32[]{:S(2)}) async-start(s8[16777216]{0:T(1024)(128)(4,1)} %bitcast.117), calls=%async_computation.26 | async-start | bytes 8388608
  514.3 11.8 %slice-start.1 = ((s8[16777216]{0:T(1024)(128)(4,1)}), s8[4194304]{0:T(1024)(128)(4,1)S(1)}, s32[]{:S(2)}) async-start(s8[16777216]{0:T(1024)(128)(4,1)} %bitcast.117), calls=%async_computation.27 | async-start | bytes 8388608
  514.3 11.8 %slice-start.2 = ((s8[16777216]{0:T(1024)(128)(4,1)}), s8[4194304]{0:T(1024)(128)(4,1)S(1)}, s32[]{:S(2)}) async-start(s8[16777216]{0:T(1024)(128)(4,1)} %bitcast.117), calls=%async_computation.28 | async-start | bytes 8388608
  519.2 6.9 slice-start.3
  621.4 7.3 copy-start.22
  621.4 7.3 copy-start.24
  621.4 7.3 copy-start.29
  621.4 7.3 copy-start.44
  636.5 267.1 %reduce-scatter.21.cloned.1.call-start = ((), (), s32[]{:S(2)}) async-start(), calls=%async_computation.24 | async-start | bytes 9437184 | tf_op jit(solution)/shard_map/reduce_scatter | solution.py:242
  650.8 405.0 %reduce-scatter.17.cloned.1.call-start = ((), (), s32[]{:S(2)}) async-start(), calls=%async_computation.22 | async-start | bytes 9437184 | tf_op jit(solution)/shard_map/reduce_scatter | solution.py:239
  661.8 90.7 %copy-start.33 = (f32[2,4]{1,0:T(2,128)S(1)}, f32[2,4]{1,0:T(2,128)}, u32[]{:S(2)}) copy-start(f32[2,4]{1,0:T(2,128)} %get-tuple-element.83) | copy-start | bytes 100
  661.8 90.7 %copy-start.34 = (f32[2,4]{1,0:T(2,128)S(1)}, f32[2,4]{1,0:T(2,128)}, u32[]{:S(2)}) copy-start(f32[2,4]{1,0:T(2,128)} %get-tuple-element.81) | copy-start | bytes 100
  661.8 241.9 %copy-start.47 = (f32[1024]{0:T(1024)S(1)}, f32[1024]{0:T(1024)}, u32[]{:S(2)}) copy-start(f32[1024]{0:T(1024)} %param.39) | copy-start | bytes 12292
  661.8 452.8 %reduce-scatter.15.cloned.1.call-start = ((), (), s32[]{:S(2)}) async-start(), calls=%async_computation.21 | async-start | bytes 327680 | tf_op jit(solution)/shard_map/reduce_scatter | solution.py:250
  662.6 453.6 %reduce-scatter.11.cloned.1.call-start = ((), (), s32[]{:S(2)}) async-start(), calls=%async_computation.19 | async-start | bytes 983040 | tf_op jit(solution)/shard_map/reduce_scatter | solution.py:247
  751.8 379.0 %reduce-scatter.23.cloned.1.call-start = ((), (), s32[]{:S(2)}) async-start(), calls=%async_computation.25 | async-start | bytes 1310720 | tf_op jit(solution)/shard_map/reduce_scatter | solution.py:256
  903.6 34.7 %copy-start.19 = (bf16[128,768]{1,0:T(8,128)(2,1)S(1)}, bf16[128,768]{1,0:T(8,128)(2,1)}, u32[]{:S(2)}) copy-start(bf16[128,768]{1,0:T(8,128)(2,1)} %param.30) | copy-start | bytes 589828
  903.6 254.7 %reduce-scatter.19.cloned.1.call-start = ((), (), s32[]{:S(2)}) async-start(), calls=%async_computation.23 | async-start | bytes 1310720 | tf_op jit(solution)/shard_map/reduce_scatter | solution.py:253
  936.6 13.7 %copy-start.48 = (f32[4]{0:T(128)}, f32[4]{0:T(128)S(1)}, u32[]{:S(2)}) copy-start(f32[4]{0:T(128)S(1)} %pmax.7) | copy-start | bytes 52
  1055.8 7.0 copy-start.26
  1055.8 8.1 copy-start.13
  (24 other events, 74.6 us)
Sparse Core Ops, SparseCore 0:
  9.6 20.8 all-gather.10
  32.0 16.8 all-gather.14
  51.1 99.0 all-gather.6
  152.2 47.4 all-gather.8
  201.6 123.4 all-gather.12
  327.1 123.1 all-gather.16
  486.8 66.3 reduce-scatter.12
  636.6 115.1 reduce-scatter.8
  755.4 148.1 reduce-scatter.20
  907.5 148.2 reduce-scatter.16
  1058.3 19.2 reduce-scatter.14
  1080.1 23.1 reduce-scatter.10
  1105.8 24.8 reduce-scatter.22
  1133.3 24.9 reduce-scatter.18
